TPU v7x, 128 devices: a whole 4x4x4 slice. The times are simulated.
128 devices in a mesh: req: 16 (over z, x), tok: 8 (over y, core).
Axes of the slice: x: 4, y: 4, z: 4, core: 2. Of those that a mesh axis runs over, the one named last changes fastest.
Arguments:
- queries: bfloat16 [8192, 2048], P('req', 'tok'), may hold values from -6 to 6
- suffix_kv: bfloat16 [8192, 2048], P('req'), may hold values from -6 to 6
- prefix_cache: bfloat16 [8192, 2048], P('req'), may hold values from -24 to 24
- q_gain: float32 [256], replicated, may hold values from 0.1 to 1.9
- k_gain: float32 [256], replicated, may hold values from 0.1 to 1.9
- lengths: int32 [16, 3], P('req'), may hold values from 1 to 256, 512 in all within a row
- group_of: int32 [16], replicated, may hold values from 0 to 1
- owner_order: int32 [16], replicated, may hold values from 0 to 15, each once
- residual: bfloat16 [8192, 2560], P('req'), may hold values from -6 to 6
- w_out: bfloat16 [2048, 2560], P('tok'), may hold values from -0.125 to 0.125
- attn_gain: float32 [2560], replicated, may hold values from 0.1 to 1.9
- ffn_in_gain: float32 [2560], replicated, may hold values from 0.1 to 1.9
- ffn_out_gain: float32 [2560], replicated, may hold values from 0.1 to 1.9
- w_gate: bfloat16 [2560, 10240], P(None, 'tok'), may hold values from -0.125 to 0.125
- w_up: bfloat16 [2560, 10240], P(None, 'tok'), may hold values from -0.125 to 0.125
- w_down: bfloat16 [10240, 2560], P('tok'), may hold values from -0.0625 to 0.0625
Outputs:
- layer_out: bfloat16 [8192, 2560], P(('req', 'tok'))
Inputs may be any that keep to these rules, and one draw needn't show every extreme that they name: The 3 lengths of each req index sum to 512; the largest is exactly 256. `owner_order`: each req index appears once; entries g * 8 to g * 8 + 7 name the holders of group g's prefix.
All inputs are finite; a program needn't handle non-finite values.
Results may differ from a plain program's by a relative error of at most 0.02.
Values may be sent and summed in bfloat16 or wider, within the bound.
A program may use at most 128 MiB of HBM per device.

v0:
```python
import jax
import jax.numpy as jnp
from jax import lax
from jax.sharding import PartitionSpec as P

H = 8
KVH = 4
HD = 256
GROUPS = 2
EPSILON = 1e-06
MASKED = -1e30


def rms_scale(values_in, gain_vec):
    return (
        values_in
        * lax.rsqrt(jnp.mean(values_in * values_in, axis=-1, keepdims=True) + EPSILON)
        * gain_vec
    )


def norm_heads(values_in, gain_vec, head_count):
    row_count = values_in.shape[0]
    shaped = values_in.astype(jnp.float32).reshape(row_count, head_count, HD)
    return rms_scale(shaped, gain_vec).astype(jnp.bfloat16).reshape(row_count, head_count * HD)


def local(
    queries,
    suffix_kv,
    prefix_cache,
    q_gain,
    k_gain,
    lengths,
    group_of,
    owner_order,
    residual,
    w_out,
    attn_gain,
    ffn_in_gain,
    ffn_out_gain,
    w_gate,
    w_up,
    w_down,
):
    req_count = lax.axis_size("req")
    tok_count = lax.axis_size("tok")
    req_index = lax.axis_index("req")
    tok_index = lax.axis_index("tok")
    row_count = queries.shape[0]
    heads_here = queries.shape[1] // HD
    head_ratio = H // KVH
    kv_first = tok_index * heads_here // head_ratio
    kv_width = KVH * HD
    own_count = req_count // GROUPS
    with jax.named_scope("prefix_gather"):
        pref_keys = lax.dynamic_slice_in_dim(prefix_cache, kv_first * HD, HD, 1)
        pref_vals = lax.dynamic_slice_in_dim(prefix_cache, kv_width + kv_first * HD, HD, 1)
        pref_kv = jnp.concatenate([pref_keys, pref_vals], axis=1)
        half_rows = pref_kv.shape[0] // 2
        core = tok_index % 2
        my_half = lax.dynamic_slice_in_dim(pref_kv, core * half_rows, half_rows, 0)
        gathered = lax.all_gather(my_half, "req", axis=0, tiled=False)
        own_group = group_of[req_index]
        owner_ids = lax.dynamic_slice_in_dim(owner_order, own_group * own_count, own_count)
        picked = jnp.take(gathered, owner_ids, axis=0).reshape(-1, 2 * HD)
        partner = [(t, t ^ 1) for t in range(tok_count)]
        swapped = lax.ppermute(picked, "tok", perm=partner)
        shared = jnp.concatenate([picked, swapped], axis=0)
    with jax.named_scope("attention"):
        query_normed = norm_heads(queries, q_gain, heads_here)
        suf_keys = norm_heads(lax.dynamic_slice_in_dim(suffix_kv, kv_first * HD, HD, 1), k_gain, 1)
        suf_vals = lax.dynamic_slice_in_dim(suffix_kv, kv_width + kv_first * HD, HD, 1)
        all_keys = jnp.concatenate([shared[:, :HD], suf_keys], axis=0)
        all_vals = jnp.concatenate([shared[:, HD:], suf_vals], axis=0)
        seg_ends = jnp.cumsum(lengths[0])
        positions = jnp.arange(row_count, dtype=jnp.int32)
        segment = jnp.sum((positions[:, None] >= seg_ends[None, :]).astype(jnp.int32), axis=1)
        causal = (segment[:, None] == segment[None, :]) & (positions[None, :] <= positions[:, None])
        visible = jnp.concatenate(
            [jnp.ones((row_count, shared.shape[0]), jnp.bool_), causal], axis=1
        )
        outputs = []
        for head_idx in range(heads_here):
            head_q = query_normed[:, head_idx * HD : (head_idx + 1) * HD]
            scores = jnp.dot(head_q, all_keys.T, preferred_element_type=jnp.float32) * HD ** (-0.5)
            scores = jnp.where(visible, scores, MASKED)
            row_max = jnp.max(scores, axis=-1, keepdims=True)
            weights = jnp.exp(scores - row_max)
            row_sum = jnp.sum(weights, axis=-1, keepdims=True)
            head_out = (
                jnp.dot(weights.astype(jnp.bfloat16), all_vals, preferred_element_type=jnp.float32)
                / row_sum
            )
            outputs.append(head_out)
        attention = jnp.concatenate(outputs, axis=1).astype(jnp.bfloat16)
    share = row_count // tok_count
    first_row = tok_index * share
    with jax.named_scope("out_projection"):
        projected = lax.psum_scatter(
            jnp.dot(attention, w_out, preferred_element_type=jnp.float32).astype(jnp.bfloat16),
            "tok",
            scatter_dimension=0,
            tiled=True,
        )
        residual_share = lax.dynamic_slice_in_dim(residual, first_row, share, 0)
        mixed_share = residual_share.astype(jnp.float32) + rms_scale(
            projected.astype(jnp.float32), attn_gain
        )
        normed_share = rms_scale(mixed_share, ffn_in_gain).astype(jnp.bfloat16)
        normed = lax.all_gather(normed_share, "tok", axis=0, tiled=True)
    with jax.named_scope("feed_forward"):
        gate = jnp.dot(normed, w_gate, preferred_element_type=jnp.float32)
        upward = jnp.dot(normed, w_up, preferred_element_type=jnp.float32)
        hidden = (jax.nn.gelu(gate, approximate=True) * upward).astype(jnp.bfloat16)
        down_share = lax.psum_scatter(
            jnp.dot(hidden, w_down, preferred_element_type=jnp.float32).astype(jnp.bfloat16),
            "tok",
            scatter_dimension=0,
            tiled=True,
        )
    return (mixed_share + rms_scale(down_share.astype(jnp.float32), ffn_out_gain)).astype(
        jnp.bfloat16
    )


def solution(mesh):
    in_specs = (
        P("req", "tok"),
        P("req", None),
        P("req", None),
        P(),
        P(),
        P("req", None),
        P(),
        P(),
        P("req", None),
        P("tok", None),
        P(),
        P(),
        P(),
        P(None, "tok"),
        P(None, "tok"),
        P("tok", None),
    )
    out_specs = P(("req", "tok"), None)
    return jax.shard_map(local, mesh=mesh, in_specs=in_specs, out_specs=out_specs, check_vma=False)
```

profile of v0, /device:TPU:0, one launch (start us, length us, event | category | flops | bytes accessed | tf_op | source)
XLA Modules:
  0.0 226.1 jit_solution(17054381908956839786)
XLA Ops:
  6.5 1.2 constant_dynamic-slice_fusion.1
  8.5 1.2 dynamic_slice.25
  11.2 52.4 %all-gather.6.cloned.1.call-done = bf16[4096,512]{1,0:T(8,128)(2,1)} async-done(((bf16[256,512]{1,0:T(8,128)(2,1)}), bf16[4096,512]{1,0:T(8,128)(2,1)}) %all-gather.6.cloned.1.call-update) | async-done | bytes 4194320 | tf_op jit(solution)/shard_map/prefix_gather/all_gather | solution.py:63
  63.7 4.2 %gather_fusion = bf16[8,256,512]{2,1,0:T(8,128)(2,1)} fusion(bf16[16,256,512]{2,1,0:T(8,128)(2,1)} %bitcast.12, s32[1024]{0:T(1024)S(1)} %pad_clamp_fusion), kind=kCustom, calls=%fused_computation | custom fusion | bytes 4194336 | tf_op jit(solution)/shard_map/prefix_gather/jit(_take)/gather | solution.py:66
  67.9 1.8 bitcast_select_fusion
  69.9 1.1 fusion.46
  71.1 1.7 constant_dynamic-slice_fusion
  72.8 1.1 fusion.43
  73.9 1.1 fusion.48
  75.3 1.4 fusion.20
  76.7 1.6 fusion.61
  78.3 3.6 %copy-done.1 = f32[512,4608]{1,0:T(8,128)} copy-done((f32[512,4608]{1,0:T(8,128)}, f32[512,4608]{1,0:T(8,128)S(1)}, u32[]{:S(2)}) %copy-start.1) | copy-done | bytes 9437208
  81.9 1.4 fusion
  83.3 8.9 %convolution_convert_fusion.1 = bf16[512,2560]{1,0:T(8,128)(2,1)} fusion(bf16[256,2560]{1,0:T(8,128)(2,1)S(1)} %copy-done, bf16[2048,512]{1,0:T(8,128)(2,1)} %collective-permute-done, bf16[2048,512]{1,0:T(8,128)(2,1)S(1)} %bitcast_select_fusion, bf16[512,256]{1,0:T(8,128)(2,1)} %constant_dynamic-slice_fusion, f32[512,4608]{1,0:T(8,128)} %copy-done.1, ...), kind=kOutput, calls=%fused_computation.8 | convolution fusion | flops 1892417536 | bytes 17829888 | tf_op jit(solution)/shard_map/out_projection/dot_general | solution.py:101
  92.3 34.4 %reduce-scatter.3.cloned.1.call-done = bf16[64,2560]{1,0:T(8,128)(2,1)} async-done(((bf16[512,2560]{1,0:T(8,128)(2,1)}), bf16[64,2560]{1,0:T(8,128)(2,1)}) %reduce-scatter.3.cloned.1.call-update) | async-done | bytes 327696 | tf_op jit(solution)/shard_map/out_projection/reduce_scatter | solution.py:100
  126.7 1.1 fusion.36
  127.9 1.4 multiply_reduce_fusion
  129.3 2.1 multiply_convert_fusion
  131.6 24.9 %all-gather.4.cloned.1.call-done = bf16[512,2560]{1,0:T(8,128)(2,1)} async-done(((bf16[64,2560]{1,0:T(8,128)(2,1)}), bf16[512,2560]{1,0:T(8,128)(2,1)}) %all-gather.4.cloned.1.call-update) | async-done | bytes 2621456 | tf_op jit(solution)/shard_map/out_projection/all_gather | solution.py:111
  156.5 8.7 %fusion.62 = f32[512,1280]{1,0:T(8,128)} fusion(bf16[512,2560]{1,0:T(8,128)(2,1)} %all-gather.4.cloned.1.call-done, bf16[2560,1280]{1,0:T(8,128)(2,1)} %param.29), kind=kOutput, calls=%fused_computation.83 | convolution fusion | flops 3355443200 | bytes 11796480 | tf_op jit(solution)/shard_map/feed_forward/dot_general | solution.py:113
  165.2 15.6 %convolution_convert_fusion = bf16[512,2560]{1,0:T(8,128)(2,1)} fusion(bf16[1280,2560]{1,0:T(8,128)(2,1)} %param.31, bf16[512,2560]{1,0:T(8,128)(2,1)} %all-gather.4.cloned.1.call-done, bf16[2560,1280]{1,0:T(8,128)(2,1)} %param.30, f32[512,1280]{1,0:T(8,128)} %fusion.62), kind=kOutput, calls=%fused_computation.7 | convolution fusion | flops 6718750720 | bytes 20971520 | tf_op jit(solution)/shard_map/feed_forward/dot_general | solution.py:117
  180.9 35.3 %reduce-scatter.5.cloned.1.call-done = bf16[64,2560]{1,0:T(8,128)(2,1)} async-done(((bf16[512,2560]{1,0:T(8,128)(2,1)}), bf16[64,2560]{1,0:T(8,128)(2,1)}) %reduce-scatter.5.cloned.1.call-update) | async-done | bytes 327696 | tf_op jit(solution)/shard_map/feed_forward/reduce_scatter | solution.py:116
  216.2 1.1 fusion.39
  217.4 2.1 fusion.42
  (42 shorter events, 2.6 us)
Async XLA Ops:
  6.5 76.8 %copy-start = (bf16[256,2560]{1,0:T(8,128)(2,1)S(1)}, bf16[256,2560]{1,0:T(8,128)(2,1)}, u32[]{:S(2)}) copy-start(bf16[256,2560]{1,0:T(8,128)(2,1)} %param.25) | copy-start | bytes 3932164
  6.5 57.1 %all-gather.6.cloned.1.call-start = ((), (), s32[]{:S(2)}) async-start(), calls=%async_computation.5 | async-start | bytes 4456448 | tf_op jit(solution)/shard_map/prefix_gather/all_gather | solution.py:63
  8.5 118.3 %reduce-scatter.3.cloned.1.call-start = ((), (), s32[]{:S(2)}) async-start(), calls=%async_computation.2 | async-start | bytes 2949120 | tf_op jit(solution)/shard_map/out_projection/reduce_scatter | solution.py:100
  67.9 1.9 copy-start.9
  67.9 6.1 %copy-start.7 = (f32[256]{0:T(256)S(1)}, f32[256]{0:T(256)}, u32[]{:S(2)}) copy-start(f32[256]{0:T(256)} %param.20) | copy-start | bytes 3076
  69.7 5.6 %collective-permute-start = (bf16[2048,512]{1,0:T(8,128)(2,1)S(1)}, bf16[2048,512]{1,0:T(8,128)(2,1)}, u32[]{:S(2)}, u32[]{:S(2)}) collective-permute-start(bf16[2048,512]{1,0:T(8,128)(2,1)S(1)} %bitcast_select_fusion), channel_id=1, source_target_pairs={{0,1},{1,0},{2,3},{3,2},{4,5},{5,4},{6,7},{7,6},{8,9},{9,8},{10,11... | collective-permute-start | bytes 6291464 | tf_op jit(solution)/shard_map/prefix_gather/ppermute | solution.py:68
  75.2 1.4 copy-start.3
  75.3 1.4 copy-start.8
  78.3 3.6 %copy-start.1 = (f32[512,4608]{1,0:T(8,128)}, f32[512,4608]{1,0:T(8,128)S(1)}, u32[]{:S(2)}) copy-start(f32[512,4608]{1,0:T(8,128)S(1)} %get-tuple-element.10) | copy-start | bytes 28311556
  92.2 35.7 %copy-start.4 = (f32[2560]{0:T(1024)S(1)}, f32[2560]{0:T(1024)}, u32[]{:S(2)}) copy-start(f32[2560]{0:T(1024)} %param.26) | copy-start | bytes 30724
  92.2 37.1 %copy-start.5 = (f32[2560]{0:T(1024)S(1)}, f32[2560]{0:T(1024)}, u32[]{:S(2)}) copy-start(f32[2560]{0:T(1024)} %param.27) | copy-start | bytes 30724
  92.2 64.3 %all-gather.4.cloned.1.call-start = ((), (), s32[]{:S(2)}) async-start(), calls=%async_computation.3 | async-start | bytes 2949120 | tf_op jit(solution)/shard_map/out_projection/all_gather | solution.py:111
  131.4 84.8 %reduce-scatter.5.cloned.1.call-start = ((), (), s32[]{:S(2)}) async-start(), calls=%async_computation.4 | async-start | bytes 2949120 | tf_op jit(solution)/shard_map/feed_forward/reduce_scatter | solution.py:116
  180.9 36.5 %copy-start.2 = (bf16[64,2560]{1,0:T(8,128)(2,1)S(1)}, bf16[64,2560]{1,0:T(8,128)(2,1)}, u32[]{:S(2)}) copy-start(bf16[64,2560]{1,0:T(8,128)(2,1)} %reduce-scatter.3.cloned.1.call-done) | copy-start | bytes 983044
  180.9 36.5 %copy-start.6 = (f32[2560]{0:T(1024)S(1)}, f32[2560]{0:T(1024)}, u32[]{:S(2)}) copy-start(f32[2560]{0:T(1024)} %param.28) | copy-start | bytes 30724
Sparse Core Ops, SparseCore 0:
  9.5 54.1 all-gather.5
  92.3 34.3 reduce-scatter.2
  131.5 24.9 all-gather.3
  181.0 35.1 reduce-scatter.4
where the time goes:
time: 227 us; the launch traced here: 226 us
  waiting for transfers between devices  147 us (65%)
  matrix products  34.8 us (15%)
  other arithmetic  17.7 us (8%)
  between operations  14 us (6%)
  local copies, waits for them, and re-layouts  12 us (5%)
    all_gather x1, waiting for transfers between devices, local(): gathered = lax.all_gather(my_half, 'req', axis=0, tiled=False)  52.4 us
    reduce_scatter x1, waiting for transfers between devices, local(): lax.psum_scatter(jnp.dot(hidden, w_down, preferred_element_type=jnp.float...  35.3 us
    reduce_scatter x1, waiting for transfers between devices, local(): lax.psum_scatter(jnp.dot(attention, w_out, preferred_element_type=jnp.flo...  34.4 us
    all_gather x1, waiting for transfers between devices, local(): normed = lax.all_gather(normed_share, 'tok', axis=0, tiled=True)  24.9 us
    dot_general x1, matrix products, local(): jnp.dot(hidden, w_down, preferred_element_type=jnp.float32)  15.6 us
    dot_general x1, matrix products, local(): jnp.dot(attention, w_out, preferred_element_type=jnp.float32)  8.88 us
    dot_general x1, matrix products, local(): gate = jnp.dot(normed, w_gate, preferred_element_type=jnp.float32)  8.71 us
    reduce_sum x5, other arithmetic, rms_scale(): jnp.mean(values_in * values_in, axis=-1, keepdims=True) + EPSILON  5.86 us
  transfers between devices with their start and end apart: 5, of which 4 were waited for; matrix products, arithmetic and copies ran while one was open for 3% of the time, Pallas kernels for 0%

commit v1 on v0

--- a/solution.py
+++ b/solution.py
@@ -108,7 +108,9 @@
             projected.astype(jnp.float32), attn_gain
         )
         normed_share = rms_scale(mixed_share, ffn_in_gain).astype(jnp.bfloat16)
-        normed = lax.all_gather(normed_share, "tok", axis=0, tiled=True)
+        normed = jnp.concatenate(
+            lax.all_to_all(jnp.stack([normed_share] * lax.axis_size("tok")), "tok", 0, 0), axis=0
+        )
     with jax.named_scope("feed_forward"):
         gate = jnp.dot(normed, w_gate, preferred_element_type=jnp.float32)
         upward = jnp.dot(normed, w_up, preferred_element_type=jnp.float32)

time: 227 us -> 236 us (1.040)
  blocking collectives: 0 us -> 35.7 us
  waiting for transfers between devices: 147 us -> 121 us
    all_to_all x0 -> x1, blocking collectives: none -> 35.7 us  [local(): lax.all_to_all(jnp.stack([normed_share] * lax.axis_size('tok')), 'tok', 0...]
    all_gather x1 -> x0, waiting for transfers between devices: 24.9 us -> none  [local(): normed = lax.all_gather(normed_share, 'tok', axis=0, tiled=True)]
    unnamed x20 -> x22, local copies, waits for them, and re-layouts: 3.66 us -> 5.19 us
  transfers between devices with their start and end apart: 5 -> 4, of which waited for: 4 -> 3; matrix products, arithmetic and copies ran while one was open for 3% -> 3% of each run, Pallas kernels for 0% -> 0%
where the time goes in v1:
time: 236 us
  waiting for transfers between devices  121 us (51%)
  blocking collectives  35.7 us (15%)
  matrix products  34 us (14%)
  other arithmetic  17 us (7%)
  between operations  14 us (6%)
  local copies, waits for them, and re-layouts  13.8 us (6%)
    all_gather x1, waiting for transfers between devices, local(): gathered = lax.all_gather(my_half, 'req', axis=0, tiled=False)  52.4 us
    all_to_all x1, blocking collectives, local(): lax.all_to_all(jnp.stack([normed_share] * lax.axis_size('tok')), 'tok', 0...  35.7 us
    reduce_scatter x1, waiting for transfers between devices, local(): lax.psum_scatter(jnp.dot(attention, w_out, preferred_element_type=jnp.flo...  34.4 us
    reduce_scatter x1, waiting for transfers between devices, local(): lax.psum_scatter(jnp.dot(hidden, w_down, preferred_element_type=jnp.float...  34.2 us
    dot_general x1, matrix products, local(): jnp.dot(hidden, w_down, preferred_element_type=jnp.float32)  15.6 us
    dot_general x1, matrix products, local(): jnp.dot(attention, w_out, preferred_element_type=jnp.float32)  8.88 us
    dot_general x1, matrix products, local(): gate = jnp.dot(normed, w_gate, preferred_element_type=jnp.float32)  7.91 us
    reduce_sum x5, other arithmetic, rms_scale(): jnp.mean(values_in * values_in, axis=-1, keepdims=True) + EPSILON  5.86 us
  transfers between devices with their start and end apart: 4, of which 3 were waited for; matrix products, arithmetic and copies ran while one was open for 3% of the time, Pallas kernels for 0%

profile of v1, /device:TPU:0, one launch (start us, length us, event | category | flops | bytes accessed | tf_op | source)
XLA Modules:
  0.0 235.7 jit_solution(7091049655828218072)
XLA Ops:
  6.5 1.2 constant_dynamic-slice_fusion.1
  8.5 1.2 dynamic_slice.25
  11.2 52.4 %all-gather.3.cloned.1.call-done = bf16[4096,512]{1,0:T(8,128)(2,1)} async-done(((bf16[256,512]{1,0:T(8,128)(2,1)}), bf16[4096,512]{1,0:T(8,128)(2,1)}) %all-gather.3.cloned.1.call-update) | async-done | bytes 4194320 | tf_op jit(solution)/shard_map/prefix_gather/all_gather | solution.py:63
  63.7 4.2 %gather_fusion = bf16[8,256,512]{2,1,0:T(8,128)(2,1)} fusion(bf16[16,256,512]{2,1,0:T(8,128)(2,1)} %bitcast.15, s32[1024]{0:T(1024)S(1)} %pad_clamp_fusion), kind=kCustom, calls=%fused_computation | custom fusion | bytes 4194336 | tf_op jit(solution)/shard_map/prefix_gather/jit(_take)/gather | solution.py:66
  67.9 1.8 bitcast_select_fusion
  69.9 1.1 fusion.46
  71.1 1.7 constant_dynamic-slice_fusion
  72.8 1.1 fusion.43
  75.3 1.4 fusion.20
  76.7 1.6 fusion.61
  78.3 3.6 %copy-done.1 = f32[512,4608]{1,0:T(8,128)} copy-done((f32[512,4608]{1,0:T(8,128)}, f32[512,4608]{1,0:T(8,128)S(1)}, u32[]{:S(2)}) %copy-start.1) | copy-done | bytes 9437208
  81.9 1.4 fusion
  83.3 8.9 %convolution_convert_fusion.1 = bf16[512,2560]{1,0:T(8,128)(2,1)} fusion(bf16[256,2560]{1,0:T(8,128)(2,1)S(1)} %copy-done, bf16[2048,512]{1,0:T(8,128)(2,1)} %collective-permute-done, bf16[2048,512]{1,0:T(8,128)(2,1)S(1)} %bitcast_select_fusion, bf16[512,256]{1,0:T(8,128)(2,1)} %constant_dynamic-slice_fusion, f32[512,4608]{1,0:T(8,128)} %copy-done.1, ...), kind=kOutput, calls=%fused_computation.8 | convolution fusion | flops 1892417536 | bytes 17829888 | tf_op jit(solution)/shard_map/out_projection/dot_general | solution.py:101
  92.3 34.4 %reduce-scatter.3.cloned.1.call-done = bf16[64,2560]{1,0:T(8,128)(2,1)} async-done(((bf16[512,2560]{1,0:T(8,128)(2,1)}), bf16[64,2560]{1,0:T(8,128)(2,1)}) %reduce-scatter.3.cloned.1.call-update) | async-done | bytes 327696 | tf_op jit(solution)/shard_map/out_projection/reduce_scatter | solution.py:100
  126.7 1.1 fusion.36
  127.9 1.4 multiply_reduce_fusion
  129.3 1.3 multiply_convert_fusion
  130.9 35.7 %all_to_all.5 = bf16[8,64,2560]{2,1,0:T(8,128)(2,1)S(1)} all-to-all(bf16[8,64,2560]{2,1,0:T(8,128)(2,1)S(1)} %stack.2), channel_id=1, replica_groups=mesh['req'=16,'tok'=8] {'tok'}, dimensions={0} | all-to-all | bytes 5242880 | tf_op jit(solution)/shard_map/out_projection/all_to_all | solution.py:112
  166.5 1.5 copy-done.3
  168.1 7.9 %fusion.62 = f32[512,1280]{1,0:T(8,128)} fusion(bf16[512,2560]{1,0:T(8,128)(2,1)S(1)} %bitcast.13, bf16[2560,1280]{1,0:T(8,128)(2,1)} %param.29), kind=kOutput, calls=%fused_computation.83 | convolution fusion | flops 3355443200 | bytes 11796480 | tf_op jit(solution)/shard_map/feed_forward/dot_general | solution.py:115
  176.0 15.6 %convolution_convert_fusion = bf16[512,2560]{1,0:T(8,128)(2,1)} fusion(bf16[1280,2560]{1,0:T(8,128)(2,1)} %param.31, bf16[512,2560]{1,0:T(8,128)(2,1)} %bitcast.14, bf16[2560,1280]{1,0:T(8,128)(2,1)} %param.30, f32[512,1280]{1,0:T(8,128)} %fusion.62), kind=kOutput, calls=%fused_computation.7 | convolution fusion | flops 6718750720 | bytes 20971520 | tf_op jit(solution)/shard_map/feed_forward/dot_general | solution.py:119
  191.6 34.2 %reduce-scatter.5.cloned.1.call-done = bf16[64,2560]{1,0:T(8,128)(2,1)} async-done(((bf16[512,2560]{1,0:T(8,128)(2,1)}), bf16[64,2560]{1,0:T(8,128)(2,1)}) %reduce-scatter.5.cloned.1.call-update) | async-done | bytes 327696 | tf_op jit(solution)/shard_map/feed_forward/reduce_scatter | solution.py:118
  225.9 1.1 fusion.39
  227.0 2.1 fusion.42
  (43 shorter events, 3.6 us)
Async XLA Ops:
  6.5 76.8 %copy-start = (bf16[256,2560]{1,0:T(8,128)(2,1)S(1)}, bf16[256,2560]{1,0:T(8,128)(2,1)}, u32[]{:S(2)}) copy-start(bf16[256,2560]{1,0:T(8,128)(2,1)} %param.25) | copy-start | bytes 3932164
  6.5 57.1 %all-gather.3.cloned.1.call-start = ((), (), s32[]{:S(2)}) async-start(), calls=%async_computation.5 | async-start | bytes 4456448 | tf_op jit(solution)/shard_map/prefix_gather/all_gather | solution.py:63
  8.5 118.3 %reduce-scatter.3.cloned.1.call-start = ((), (), s32[]{:S(2)}) async-start(), calls=%async_computation.3 | async-start | bytes 2949120 | tf_op jit(solution)/shard_map/out_projection/reduce_scatter | solution.py:100
  67.9 1.9 copy-start.10
  67.9 6.1 %copy-start.8 = (f32[256]{0:T(256)S(1)}, f32[256]{0:T(256)}, u32[]{:S(2)}) copy-start(f32[256]{0:T(256)} %param.20) | copy-start | bytes 3076
  69.7 5.6 %collective-permute-start = (bf16[2048,512]{1,0:T(8,128)(2,1)S(1)}, bf16[2048,512]{1,0:T(8,128)(2,1)}, u32[]{:S(2)}, u32[]{:S(2)}) collective-permute-start(bf16[2048,512]{1,0:T(8,128)(2,1)S(1)} %bitcast_select_fusion), channel_id=1, source_target_pairs={{0,1},{1,0},{2,3},{3,2},{4,5},{5,4},{6,7},{7,6},{8,9},{9,8},{10,11... | collective-permute-start | bytes 6291464 | tf_op jit(solution)/shard_map/prefix_gather/ppermute | solution.py:68
  75.2 1.4 copy-start.4
  75.3 1.4 copy-start.9
  78.3 3.6 %copy-start.1 = (f32[512,4608]{1,0:T(8,128)}, f32[512,4608]{1,0:T(8,128)S(1)}, u32[]{:S(2)}) copy-start(f32[512,4608]{1,0:T(8,128)S(1)} %get-tuple-element.10) | copy-start | bytes 28311556
  92.2 35.7 %copy-start.5 = (f32[2560]{0:T(1024)S(1)}, f32[2560]{0:T(1024)}, u32[]{:S(2)}) copy-start(f32[2560]{0:T(1024)} %param.26) | copy-start | bytes 30724
  92.2 37.1 %copy-start.6 = (f32[2560]{0:T(1024)S(1)}, f32[2560]{0:T(1024)}, u32[]{:S(2)}) copy-start(f32[2560]{0:T(1024)} %param.27) | copy-start | bytes 30724
  92.2 133.6 %reduce-scatter.5.cloned.1.call-start = ((), (), s32[]{:S(2)}) async-start(), calls=%async_computation.4 | async-start | bytes 2949120 | tf_op jit(solution)/shard_map/feed_forward/reduce_scatter | solution.py:118
  166.5 1.5 copy-start.3
  191.6 35.4 %copy-start.2 = (bf16[64,2560]{1,0:T(8,128)(2,1)S(1)}, bf16[64,2560]{1,0:T(8,128)(2,1)}, u32[]{:S(2)}) copy-start(bf16[64,2560]{1,0:T(8,128)(2,1)} %reduce-scatter.3.cloned.1.call-done) | copy-start | bytes 983044
  191.6 35.4 %copy-start.7 = (f32[2560]{0:T(1024)S(1)}, f32[2560]{0:T(1024)}, u32[]{:S(2)}) copy-start(f32[2560]{0:T(1024)} %param.28) | copy-start | bytes 30724
Sparse Core Ops, SparseCore 0:
  9.5 54.1 all-gather.2
  92.3 34.3 reduce-scatter.2
  191.8 34.0 reduce-scatter.4
